TPU v7x, 32 devices: a whole 2x2x4 slice. The times are simulated.
32 devices in a mesh: group: 4 (over y, x), leaf: 8 (over z, core).
Axes of the slice: x: 2, y: 2, z: 4, core: 2. Of those that a mesh axis runs over, the one named last changes fastest.
Arguments:
- points: bfloat16 [65536, 64], P(('group', 'leaf')), may hold values from -1.1953125 to 1.1953125
- ordering: int32 [32, 2048], P(('group', 'leaf')), may hold values from 0 to 2047, each once within a row
- iterate: float32 [65536, 128], P(('group', 'leaf')), may hold values from -6 to 6
- target: float32 [65536, 128], P(('group', 'leaf')), may hold values from -18 to 18
- step_size: float32 [128], replicated, may hold values from 0.1 to 0.5
- leaf_basis: bfloat16 [65536, 256], P(('group', 'leaf')), may hold values from -0.125 to 0.125
- transfer: bfloat16 [32, 256, 256], P(('group', 'leaf')), may hold values from -0.375 to 0.375
- leaf_skeleton: bfloat16 [32, 256, 64], P(('group', 'leaf')), may hold values from -0.8984375 to 0.8984375
- cluster_skeleton: bfloat16 [4, 256, 64], P('group'), may hold values from -1.1953125 to 1.1953125
- near_table: int32 [32, 8], P(('group', 'leaf')), may hold values from 0 to 1, as said below
- far_table: int32 [32, 8], P(('group', 'leaf')), may hold values from 0 to 1, as said below
- cluster_far: int32 [4, 4], P('group'), may hold values from 0 to 1, as said below
Outputs:
- updated: float32 [65536, 128], P(('group', 'leaf'))
Inputs may be any that keep to these rules, and one draw needn't show every extreme that they name: `near_table`: entries 0 or 1; each leaf's own place is 1; a 1 stands only at places at most 3 away from the leaf's own place; each row has at most 7 ones, and some row exactly 7. `far_table`: entries 0 or 1, never 1 where near_table is 1. `cluster_far`: entries 0 or 1, zero on the diagonal. `ordering`: each row is a permutation.
All inputs are finite; a program needn't handle non-finite values.
Results may differ from a plain program's by a relative error of at most 0.0044.
Values may be sent and summed in bfloat16 or wider, within the bound.
No kernel may reach another device: no remote copies, remote signals or barrier semaphores. Data moves between devices by JAX's collectives and lax.ppermute only.
A program may use at most 128 MiB of HBM per device.

v0:
```python
import jax
import jax.numpy as jnp
from jax import lax
from jax.sharding import PartitionSpec as P

NEAR_MOST = 7


def passed_along(block, axis, distance):
    devices = range(lax.axis_size(axis))
    route = [(i - distance, i) for i in devices if i - distance in devices]
    return lax.ppermute(block, axis, route)


def kernel_tile(left, right):
    left_f = left.astype(jnp.float32)
    right_f = right.astype(jnp.float32)
    left_sq = jnp.sum(left_f * left_f, axis=1)
    right_sq = jnp.sum(right_f * right_f, axis=1)
    inner = lax.dot_general(
        left, right, (((1,), (1,)), ((), ())), preferred_element_type=jnp.float32
    )
    return jnp.exp(-(left_sq[:, None] + right_sq[None, :] - 2.0 * inner)).astype(jnp.bfloat16)


def body(
    points,
    ordering,
    iterate,
    target,
    step_size,
    leaf_basis,
    transfer,
    leaf_skeleton,
    cluster_skeleton,
    near_table,
    far_table,
    cluster_far,
):
    leaf_rows = points.shape[0]
    point_cols = points.shape[1]
    rhs_cols = iterate.shape[1]
    rank_cols = leaf_basis.shape[1]
    rounded = iterate.astype(jnp.bfloat16)
    coeffs = lax.dot_general(
        leaf_basis, rounded, (((0,), (0,)), ((), ())), preferred_element_type=jnp.float32
    ).astype(jnp.bfloat16)
    near_row = near_table[0]
    far_row = far_table[0]
    own_transfer = transfer[0]
    reach = (NEAR_MOST - 1) // 2
    joined = jnp.concatenate([points, rounded], axis=1)
    below_blocks = []
    above_blocks = []
    passing_below = joined
    passing_above = joined
    for distance in range(1, reach + 1):
        passing_below = passed_along(passing_below, "leaf", 1)
        passing_above = passed_along(passing_above, "leaf", -1)
        below_blocks.append(passing_below)
        above_blocks.append(passing_above)
    padded = jnp.concatenate(below_blocks[::-1] + [joined] + above_blocks, axis=0)
    myself = lax.axis_index("leaf")
    cluster_size = near_row.shape[0]

    def window_visit(position, summed):
        place = myself + position - reach
        inside = (place >= 0) & (place < cluster_size)
        listed = lax.dynamic_index_in_dim(
            near_row, jnp.clip(place, 0, cluster_size - 1), 0, keepdims=False
        )
        block = lax.dynamic_slice_in_dim(padded, position * leaf_rows, leaf_rows, 0)
        other_points = block[:, :point_cols]
        other_values = block[:, point_cols:]

        def include(current):
            return current + jnp.dot(
                kernel_tile(points, other_points), other_values, preferred_element_type=jnp.float32
            )

        return lax.cond(inside & (listed > 0), include, lambda current: current, summed)

    near_sum = lax.fori_loop(
        0, 2 * reach + 1, window_visit, jnp.zeros((leaf_rows, rhs_cols), jnp.float32)
    )

    def far_visit(skeletons, values):

        def visit(position, summed):
            listed = lax.dynamic_index_in_dim(far_row, position, 0, keepdims=False)

            def include(current):
                return current + jnp.dot(
                    kernel_tile(leaf_skeleton[0], skeletons[position]),
                    values[position],
                    preferred_element_type=jnp.float32,
                )

            return lax.cond(listed > 0, include, lambda current: current, summed)

        return visit

    empty_far = jnp.zeros((rank_cols, rhs_cols), jnp.float32)
    skeletons = lax.all_gather(leaf_skeleton, "leaf", axis=0, tiled=True)
    values = lax.all_gather(coeffs[None], "leaf", axis=0, tiled=True)
    far_sum = lax.fori_loop(0, skeletons.shape[0], far_visit(skeletons, values), empty_far)
    upward_terms = lax.dot_general(
        own_transfer, coeffs, (((0,), (0,)), ((), ())), preferred_element_type=jnp.float32
    )
    upper = lax.psum(upward_terms, "leaf").astype(jnp.bfloat16)
    cluster_row = cluster_far[0]
    skeletons = lax.all_gather(cluster_skeleton, "group", axis=0, tiled=True)
    values = lax.all_gather(upper[None], "group", axis=0, tiled=True)

    def visit(position, summed):
        listed = lax.dynamic_index_in_dim(cluster_row, position, 0, keepdims=False)

        def include(current):
            return current + jnp.dot(
                kernel_tile(cluster_skeleton[0], skeletons[position]),
                values[position],
                preferred_element_type=jnp.float32,
            )

        return lax.cond(listed > 0, include, lambda current: current, summed)

    lower = lax.fori_loop(0, skeletons.shape[0], visit, empty_far).astype(jnp.bfloat16)
    local = (far_sum + jnp.dot(own_transfer, lower, preferred_element_type=jnp.float32)).astype(
        jnp.bfloat16
    )
    image = jnp.dot(leaf_basis, local, preferred_element_type=jnp.float32) + near_sum
    sorted_target = target[ordering[0]]
    return iterate + step_size[None, :] * (sorted_target - image)


def solution(mesh):
    return jax.shard_map(
        body,
        mesh=mesh,
        in_specs=(
            P(("group", "leaf"), None),
            P(("group", "leaf"), None),
            P(("group", "leaf"), None),
            P(("group", "leaf"), None),
            P(),
            P(("group", "leaf"), None),
            P(("group", "leaf"), None, None),
            P(("group", "leaf"), None, None),
            P("group", None, None),
            P(("group", "leaf"), None),
            P(("group", "leaf"), None),
            P("group", None),
        ),
        out_specs=P(("group", "leaf"), None),
        check_vma=False,
    )
```

profile of v0, /device:TPU:15, one launch (start us, length us, event | category | flops | bytes accessed | tf_op | source)
XLA Modules:
  0.0 278.6 jit_solution(15546868874311557150)
XLA Ops:
  4.6 3.9 %collective-permute-start = (bf16[2048,192]{0,1:T(8,128)(2,1)}, bf16[2048,192]{0,1:T(8,128)(2,1)}, u32[]{:S(2)}, u32[]{:S(2)}) collective-permute-start(bf16[2048,192]{0,1:T(8,128)(2,1)} %pad_maximum_fusion), channel_id=1, source_target_pairs={{0,1},{1,2},{2,3},{3,4},{4,5},{5,6},{6,7},{8,9},{9,10},{10,11},{11... | collective-permute-start | bytes 2359304 | tf_op jit(solution)/shard_map/ppermute | solution.py:12
  10.4 7.3 %collective-permute-done = bf16[2048,192]{0,1:T(8,128)(2,1)} collective-permute-done((bf16[2048,192]{0,1:T(8,128)(2,1)}, bf16[2048,192]{0,1:T(8,128)(2,1)}, u32[]{:S(2)}, u32[]{:S(2)}) %collective-permute-start) | collective-permute-done | bytes 786464 | tf_op jit(solution)/shard_map/ppermute | solution.py:12
  17.7 4.4 %collective-permute-start.1 = (bf16[2048,192]{0,1:T(8,128)(2,1)}, bf16[2048,192]{0,1:T(8,128)(2,1)}, u32[]{:S(2)}, u32[]{:S(2)}) collective-permute-start(bf16[2048,192]{0,1:T(8,128)(2,1)} %collective-permute-done), channel_id=1, source_target_pairs={{0,1},{1,2},{2,3},{3,4},{4,5},{5,6},{6,7},{8,9},{9,10},{10,11},{11... | collective-permute-start | bytes 2359304 | tf_op jit(solution)/shard_map/ppermute | solution.py:12
  22.8 25.1 %all-reduce.1 = bf16[256,128]{0,1:T(8,128)(2,1)S(1)} all-reduce(f32[256,128]{0,1:T(8,128)S(1)} %convolution_bitcast_fusion.2), channel_id=1, replica_groups=mesh['group'=4,'leaf'=8] {'leaf'}, use_global_device_ids=true, to_apply=%region_6.7 | all-reduce | flops 32768 | bytes 196608 | tf_op jit(solution)/shard_map/psum | solution.py:110
  47.9 17.8 %all-gather = bf16[2048,128]{1,0:T(8,128)(2,1)} all-gather(bf16[256,128]{1,0:T(8,128)(2,1)S(1)} %convolution_convert_fusion), channel_id=2, replica_groups=mesh['group'=4,'leaf'=8] {'leaf'}, dimensions={0}, use_global_device_ids=true | all-gather | bytes 589824 | tf_op jit(solution)/shard_map/all_gather | solution.py:105
  67.8 4.1 %collective-permute-start.2 = (bf16[2048,192]{0,1:T(8,128)(2,1)}, bf16[2048,192]{0,1:T(8,128)(2,1)}, u32[]{:S(2)}, u32[]{:S(2)}) collective-permute-start(bf16[2048,192]{0,1:T(8,128)(2,1)} %collective-permute-done.1), channel_id=1, source_target_pairs={{0,1},{1,2},{2,3},{3,4},{4,5},{5,6},{6,7},{8,9},{9,10},{10,11},{11... | collective-permute-start | bytes 2359304 | tf_op jit(solution)/shard_map/ppermute | solution.py:12
  71.9 20.0 %all_gather.12 = bf16[8,256,64]{1,2,0:T(8,128)(2,1)} all-gather(bf16[1,256,64]{1,2,0:T(8,128)(2,1)S(1)} %copy-done.8), channel_id=1, replica_groups=mesh['group'=4,'leaf'=8] {'leaf'}, dimensions={0}, use_global_device_ids=true | all-gather | bytes 294912 | tf_op jit(solution)/shard_map/all_gather | solution.py:104
  95.7 17.8 %while.50 = (s32[]{:T(128)}, f32[256,128]{1,0:T(8,128)}, s32[8]{0:T(128)}, bf16[1,256,64]{2,1,0:T(8,128)(2,1)S(1)}, bf16[8,256,64]{2,1,0:T(8,128)(2,1)}, /*index...) while((s32[]{:T(128)}, f32[256,128]{1,0:T(8,128)}, s32[8]{0:T(128)}, bf16[1,256,64]{2,1,0:T(8,128)(2,1)S(1)}, ...), condition=%wide.region_5.6_spmd, body=%wide.region_0.5_spmd.sunk | while | flops 25624072 | bytes 496837 | solution.py:106
  110.4 3.1 %conditional.6 = (f32[256,128]{1,0:T(8,128)}) conditional(s32[]{:T(128)} %bitcast.109, f32[256,128]{1,0:T(8,128)} %get-tuple-element.740, (bf16[1,256,64]{2,1,0:T(8,128)(2,1)S(1)}, s32[]{:T(128)}, bf16[8,256,64]{2,1,0:T(8,128)(2,1)}, bf16[8,256,128]{2,1,0:T(8,128)(2,1)}, f32[256,128]{1,0:T(8,128)}) %tuple.135), branch_computations={%region_1.1_spmd, %region_2.4_spmd} | conditional | flops 25624068 | bytes 496686 | solution.py:99
  115.2 13.8 %all-gather.1 = bf16[1024,128]{0,1:T(8,128)(2,1)} all-gather(bf16[256,128]{0,1:T(8,128)(2,1)S(1)} %all-reduce.1), channel_id=3, replica_groups=mesh['group'=4,'leaf'=8] {'group'}, dimensions={0}, use_global_device_ids=true | all-gather | bytes 327680 | tf_op jit(solution)/shard_map/all_gather | solution.py:113
  131.6 7.2 %all_gather.14 = bf16[4,256,64]{1,2,0:T(8,128)(2,1)} all-gather(bf16[1,256,64]{1,2,0:T(8,128)(2,1)} %param.32), channel_id=1, replica_groups=mesh['group'=4,'leaf'=8] {'group'}, dimensions={0}, use_global_device_ids=true | all-gather | bytes 163840 | tf_op jit(solution)/shard_map/all_gather | solution.py:112
  140.6 7.6 %gather_fusion = f32[2048,128]{1,0:T(8,128)} fusion(f32[2048,128]{1,0:T(8,128)S(1)} %copy-done.1, s32[2048]{0:T(1024)S(1)} %broadcast_clamp_fusion), kind=kCustom, calls=%fused_computation | custom fusion | bytes 2105344 | tf_op jit(solution)/shard_map/gather | solution.py:132
  148.2 2.6 copy.45
  150.8 9.8 %while.51 = (s32[]{:T(128)}, f32[256,128]{1,0:T(8,128)S(1)}, s32[4]{0:T(128)S(1)}, bf16[1,256,64]{2,1,0:T(8,128)(2,1)S(1)}, bf16[4,256,64]{2,1,0:T(8,128)(2,1)},...) while((s32[]{:T(128)}, f32[256,128]{1,0:T(8,128)S(1)}, s32[4]{0:T(128)S(1)}, ...), condition=%wide.region_12.13_spmd, body=%wide.region_7.12_spmd.sunk | while | flops 25624072 | bytes 496837 | solution.py:127
  160.7 9.4 %collective-permute-start.5 = (bf16[2048,192]{0,1:T(8,128)(2,1)}, bf16[2048,192]{0,1:T(8,128)(2,1)S(1)}, u32[]{:S(2)}, u32[]{:S(2)}) collective-permute-start(bf16[2048,192]{0,1:T(8,128)(2,1)} %collective-permute-done.4), channel_id=1, source_target_pairs={{1,0},{2,1},{3,2},{4,3},{5,4},{6,5},{7,6},{9,8},{10,9},{11,10},{12... | collective-permute-start | bytes 2359304 | tf_op jit(solution)/shard_map/ppermute | solution.py:12
  182.8 9.2 %copy.43 = bf16[14336,192]{1,0:T(8,128)(2,1)} copy(bf16[14336,192]{0,1:T(8,128)(2,1)} %constant_dynamic-update-slice_fusion) | data formatting | bytes 11010048 | tf_op jit(solution)/shard_map/while | solution.py:83
  193.2 77.1 %while.52 = (s32[]{:T(128)}, f32[2048,128]{1,0:T(8,128)}, s32[]{:T(128)}, s32[8]{0:T(128)S(1)}, bf16[2048,64]{1,0:T(8,128)(2,1)S(1)}, /*index=5*/bf16[14336,192]...) while((s32[]{:T(128)}, f32[2048,128]{1,0:T(8,128)}, ...), condition=%wide.region_18.19_spmd, body=%wide.region_13.18_spmd.sunk | while | flops 1632628736 | bytes 3966781 | solution.py:83
  194.5 9.7 %conditional.8 = (f32[2048,128]{1,0:T(8,128)}) conditional(s32[]{:T(128)} %convert_element_type.116, f32[2048,128]{1,0:T(8,128)} %get-tuple-element.708, (bf16[2048,64]{1,0:T(8,128)(2,1)S(1)}, s32[]{:T(128)}, bf16[14336,192]{1,0:T(8,128)(2,1)}, f32[2048,128]{1,0:T(8,128)}) %tuple.139), branch_computations={%region_14.14_spmd, %region_15.17_spmd} | conditional | flops 1632628736 | bytes 3966534 | solution.py:81
  196.2 8.0 %convolution_add_fusion = f32[2048,128]{1,0:T(8,128)} fusion(f32[2048,128]{1,0:T(8,128)} %get-tuple-element.471, bf16[2048,64]{1,0:T(8,128)(2,1)S(1)} %get-tuple-element.472, f32[2048]{0:T(1024)S(1)} %get-tuple-element.582, f32[2048]{0:T(1024)S(1)} %get-tuple-element.583, bf16[14336,192]{1,0:T(8,128)(2,1)} %get-tuple-element.473, s32[]{:T(128)S(6)} %select_n.45, ...), kind=kOutput, calls=%fused_computation.47 | convolution fusion | flops 1631846400 | bytes 3425792 | tf_op jit(solution)/shard_map/while/body/eval_jaxpr/cond/branch_1_fun/dot_general | solution.py:77
  205.5 9.7 %conditional.8 = (f32[2048,128]{1,0:T(8,128)}) conditional(s32[]{:T(128)} %convert_element_type.116, f32[2048,128]{1,0:T(8,128)} %get-tuple-element.708, (bf16[2048,64]{1,0:T(8,128)(2,1)S(1)}, s32[]{:T(128)}, bf16[14336,192]{1,0:T(8,128)(2,1)}, f32[2048,128]{1,0:T(8,128)}) %tuple.139), branch_computations={%region_14.14_spmd, %region_15.17_spmd} | conditional | flops 1632628736 | bytes 3966534 | solution.py:81
  207.2 8.0 %convolution_add_fusion = f32[2048,128]{1,0:T(8,128)} fusion(f32[2048,128]{1,0:T(8,128)} %get-tuple-element.471, bf16[2048,64]{1,0:T(8,128)(2,1)S(1)} %get-tuple-element.472, f32[2048]{0:T(1024)S(1)} %get-tuple-element.582, f32[2048]{0:T(1024)S(1)} %get-tuple-element.583, bf16[14336,192]{1,0:T(8,128)(2,1)} %get-tuple-element.473, s32[]{:T(128)S(6)} %select_n.45, ...), kind=kOutput, calls=%fused_computation.47 | convolution fusion | flops 1631846400 | bytes 3425792 | tf_op jit(solution)/shard_map/while/body/eval_jaxpr/cond/branch_1_fun/dot_general | solution.py:77
  216.5 9.7 %conditional.8 = (f32[2048,128]{1,0:T(8,128)}) conditional(s32[]{:T(128)} %convert_element_type.116, f32[2048,128]{1,0:T(8,128)} %get-tuple-element.708, (bf16[2048,64]{1,0:T(8,128)(2,1)S(1)}, s32[]{:T(128)}, bf16[14336,192]{1,0:T(8,128)(2,1)}, f32[2048,128]{1,0:T(8,128)}) %tuple.139), branch_computations={%region_14.14_spmd, %region_15.17_spmd} | conditional | flops 1632628736 | bytes 3966534 | solution.py:81
  218.2 8.0 %convolution_add_fusion = f32[2048,128]{1,0:T(8,128)} fusion(f32[2048,128]{1,0:T(8,128)} %get-tuple-element.471, bf16[2048,64]{1,0:T(8,128)(2,1)S(1)} %get-tuple-element.472, f32[2048]{0:T(1024)S(1)} %get-tuple-element.582, f32[2048]{0:T(1024)S(1)} %get-tuple-element.583, bf16[14336,192]{1,0:T(8,128)(2,1)} %get-tuple-element.473, s32[]{:T(128)S(6)} %select_n.45, ...), kind=kOutput, calls=%fused_computation.47 | convolution fusion | flops 1631846400 | bytes 3425792 | tf_op jit(solution)/shard_map/while/body/eval_jaxpr/cond/branch_1_fun/dot_general | solution.py:77
  227.5 9.7 %conditional.8 = (f32[2048,128]{1,0:T(8,128)}) conditional(s32[]{:T(128)} %convert_element_type.116, f32[2048,128]{1,0:T(8,128)} %get-tuple-element.708, (bf16[2048,64]{1,0:T(8,128)(2,1)S(1)}, s32[]{:T(128)}, bf16[14336,192]{1,0:T(8,128)(2,1)}, f32[2048,128]{1,0:T(8,128)}) %tuple.139), branch_computations={%region_14.14_spmd, %region_15.17_spmd} | conditional | flops 1632628736 | bytes 3966534 | solution.py:81
  229.2 8.0 %convolution_add_fusion = f32[2048,128]{1,0:T(8,128)} fusion(f32[2048,128]{1,0:T(8,128)} %get-tuple-element.471, bf16[2048,64]{1,0:T(8,128)(2,1)S(1)} %get-tuple-element.472, f32[2048]{0:T(1024)S(1)} %get-tuple-element.582, f32[2048]{0:T(1024)S(1)} %get-tuple-element.583, bf16[14336,192]{1,0:T(8,128)(2,1)} %get-tuple-element.473, s32[]{:T(128)S(6)} %select_n.45, ...), kind=kOutput, calls=%fused_computation.47 | convolution fusion | flops 1631846400 | bytes 3425792 | tf_op jit(solution)/shard_map/while/body/eval_jaxpr/cond/branch_1_fun/dot_general | solution.py:77
  238.5 9.7 %conditional.8 = (f32[2048,128]{1,0:T(8,128)}) conditional(s32[]{:T(128)} %convert_element_type.116, f32[2048,128]{1,0:T(8,128)} %get-tuple-element.708, (bf16[2048,64]{1,0:T(8,128)(2,1)S(1)}, s32[]{:T(128)}, bf16[14336,192]{1,0:T(8,128)(2,1)}, f32[2048,128]{1,0:T(8,128)}) %tuple.139), branch_computations={%region_14.14_spmd, %region_15.17_spmd} | conditional | flops 1632628736 | bytes 3966534 | solution.py:81
  240.2 8.0 %convolution_add_fusion = f32[2048,128]{1,0:T(8,128)} fusion(f32[2048,128]{1,0:T(8,128)} %get-tuple-element.471, bf16[2048,64]{1,0:T(8,128)(2,1)S(1)} %get-tuple-element.472, f32[2048]{0:T(1024)S(1)} %get-tuple-element.582, f32[2048]{0:T(1024)S(1)} %get-tuple-element.583, bf16[14336,192]{1,0:T(8,128)(2,1)} %get-tuple-element.473, s32[]{:T(128)S(6)} %select_n.45, ...), kind=kOutput, calls=%fused_computation.47 | convolution fusion | flops 1631846400 | bytes 3425792 | tf_op jit(solution)/shard_map/while/body/eval_jaxpr/cond/branch_1_fun/dot_general | solution.py:77
  249.5 9.7 %conditional.8 = (f32[2048,128]{1,0:T(8,128)}) conditional(s32[]{:T(128)} %convert_element_type.116, f32[2048,128]{1,0:T(8,128)} %get-tuple-element.708, (bf16[2048,64]{1,0:T(8,128)(2,1)S(1)}, s32[]{:T(128)}, bf16[14336,192]{1,0:T(8,128)(2,1)}, f32[2048,128]{1,0:T(8,128)}) %tuple.139), branch_computations={%region_14.14_spmd, %region_15.17_spmd} | conditional | flops 1632628736 | bytes 3966534 | solution.py:81
  251.2 8.1 %convolution_add_fusion = f32[2048,128]{1,0:T(8,128)} fusion(f32[2048,128]{1,0:T(8,128)} %get-tuple-element.471, bf16[2048,64]{1,0:T(8,128)(2,1)S(1)} %get-tuple-element.472, f32[2048]{0:T(1024)S(1)} %get-tuple-element.582, f32[2048]{0:T(1024)S(1)} %get-tuple-element.583, bf16[14336,192]{1,0:T(8,128)(2,1)} %get-tuple-element.473, s32[]{:T(128)S(6)} %select_n.45, ...), kind=kOutput, calls=%fused_computation.47 | convolution fusion | flops 1631846400 | bytes 3425792 | tf_op jit(solution)/shard_map/while/body/eval_jaxpr/cond/branch_1_fun/dot_general | solution.py:77
  260.5 9.8 %conditional.8 = (f32[2048,128]{1,0:T(8,128)}) conditional(s32[]{:T(128)} %convert_element_type.116, f32[2048,128]{1,0:T(8,128)} %get-tuple-element.708, (bf16[2048,64]{1,0:T(8,128)(2,1)S(1)}, s32[]{:T(128)}, bf16[14336,192]{1,0:T(8,128)(2,1)}, f32[2048,128]{1,0:T(8,128)}) %tuple.139), branch_computations={%region_14.14_spmd, %region_15.17_spmd} | conditional | flops 1632628736 | bytes 3966534 | solution.py:81
  262.2 8.1 %convolution_add_fusion = f32[2048,128]{1,0:T(8,128)} fusion(f32[2048,128]{1,0:T(8,128)} %get-tuple-element.471, bf16[2048,64]{1,0:T(8,128)(2,1)S(1)} %get-tuple-element.472, f32[2048]{0:T(1024)S(1)} %get-tuple-element.582, f32[2048]{0:T(1024)S(1)} %get-tuple-element.583, bf16[14336,192]{1,0:T(8,128)(2,1)} %get-tuple-element.473, s32[]{:T(128)S(6)} %select_n.45, ...), kind=kOutput, calls=%fused_computation.47 | convolution fusion | flops 1631846400 | bytes 3425792 | tf_op jit(solution)/shard_map/while/body/eval_jaxpr/cond/branch_1_fun/dot_general | solution.py:77
  272.9 3.2 %fusion.56 = f32[2048,128]{0,1:T(8,128)} fusion(f32[2048,128]{0,1:T(8,128)S(1)} %copy-done.3, f32[2048,128]{0,1:T(8,128)} %copy.45, f32[2048,128]{0,1:T(8,128)} %copy.44, bf16[2048,256]{1,0:T(8,128)(2,1)S(1)} %copy-done, f32[256,128]{0,1:T(8,128)S(1)} %copy-done.7, f32[128]{0:T(128)S(1)} %copy-done.10, bf16[1,256,256]{2,1,0:T(8,128)(2,1)S(1)} %copy-done.6, ...), kind=kOutput, calls=%fused_computation.58 | convolution fusion | flops 152141824 | bytes 5636608 | tf_op jit(solution)/shard_map/dot_general | solution.py:131
  (102 shorter events, 78.9 us)
Async XLA Ops:
  0.0 22.1 %copy-start = (bf16[2048,256]{1,0:T(8,128)(2,1)S(1)}, bf16[2048,256]{1,0:T(8,128)(2,1)}, u32[]{:S(2)}) copy-start(bf16[2048,256]{1,0:T(8,128)(2,1)} %param.29) | copy-start | bytes 3145732
  0.0 91.9 %copy-start.4 = (bf16[2048,64]{0,1:T(8,128)(2,1)S(1)}, bf16[2048,64]{0,1:T(8,128)(2,1)}, u32[]{:S(2)}) copy-start(bf16[2048,64]{0,1:T(8,128)(2,1)} %param.24) | copy-start | bytes 786436
  0.0 22.6 %copy-start.5 = (bf16[1,256,256]{2,1,0:T(8,128)(2,1)S(1)}, bf16[1,256,256]{2,1,0:T(8,128)(2,1)}, u32[]{:S(2)}) copy-start(bf16[1,256,256]{2,1,0:T(8,128)(2,1)} %param.30) | copy-start | bytes 393220
  0.0 71.9 %copy-start.8 = (bf16[1,256,64]{1,2,0:T(8,128)(2,1)S(1)}, bf16[1,256,64]{1,2,0:T(8,128)(2,1)}, u32[]{:S(2)}) copy-start(bf16[1,256,64]{1,2,0:T(8,128)(2,1)} %param.31) | copy-start | bytes 98308
  1.7 1.0 copy-start.2
  2.7 137.9 %copy-start.9 = (s32[1,2048]{1,0:T(1,128)S(1)}, s32[1,2048]{1,0:T(1,128)}, u32[]{:S(2)}) copy-start(s32[1,2048]{1,0:T(1,128)} %param.25) | copy-start | bytes 24580
  4.6 136.0 %copy-start.1 = (f32[2048,128]{1,0:T(8,128)S(1)}, f32[2048,128]{1,0:T(8,128)}, u32[]{:S(2)}) copy-start(f32[2048,128]{1,0:T(8,128)} %param.27) | copy-start | bytes 3145732
  4.6 13.1 %collective-permute-start = (bf16[2048,192]{0,1:T(8,128)(2,1)}, bf16[2048,192]{0,1:T(8,128)(2,1)}, u32[]{:S(2)}, u32[]{:S(2)}) collective-permute-start(bf16[2048,192]{0,1:T(8,128)(2,1)} %pad_maximum_fusion), channel_id=1, source_target_pairs={{0,1},{1,2},{2,3},{3,4},{4,5},{5,6},{6,7},{8,9},{9,10},{10,11},{11... | collective-permute-start | bytes 2359304 | tf_op jit(solution)/shard_map/ppermute | solution.py:12
  8.5 57.3 %collective-permute-start.3 = (bf16[2048,192]{0,1:T(8,128)(2,1)}, bf16[2048,192]{0,1:T(8,128)(2,1)}, u32[]{:S(2)}, u32[]{:S(2)}) collective-permute-start(bf16[2048,192]{0,1:T(8,128)(2,1)} %pad_maximum_fusion), channel_id=1, source_target_pairs={{1,0},{2,1},{3,2},{4,3},{5,4},{6,5},{7,6},{9,8},{10,9},{11,10},{12... | collective-permute-start | bytes 2359304 | tf_op jit(solution)/shard_map/ppermute | solution.py:12
  17.7 50.1 %collective-permute-start.1 = (bf16[2048,192]{0,1:T(8,128)(2,1)}, bf16[2048,192]{0,1:T(8,128)(2,1)}, u32[]{:S(2)}, u32[]{:S(2)}) collective-permute-start(bf16[2048,192]{0,1:T(8,128)(2,1)} %collective-permute-done), channel_id=1, source_target_pairs={{0,1},{1,2},{2,3},{3,4},{4,5},{5,6},{6,7},{8,9},{9,10},{10,11},{11... | collective-permute-start | bytes 2359304 | tf_op jit(solution)/shard_map/ppermute | solution.py:12
  65.8 94.9 %collective-permute-start.4 = (bf16[2048,192]{0,1:T(8,128)(2,1)}, bf16[2048,192]{0,1:T(8,128)(2,1)}, u32[]{:S(2)}, u32[]{:S(2)}) collective-permute-start(bf16[2048,192]{0,1:T(8,128)(2,1)} %collective-permute-done.3), channel_id=1, source_target_pairs={{1,0},{2,1},{3,2},{4,3},{5,4},{6,5},{7,6},{9,8},{10,9},{11,10},{12... | collective-permute-start | bytes 2359304 | tf_op jit(solution)/shard_map/ppermute | solution.py:12
  67.8 102.2 %collective-permute-start.2 = (bf16[2048,192]{0,1:T(8,128)(2,1)}, bf16[2048,192]{0,1:T(8,128)(2,1)}, u32[]{:S(2)}, u32[]{:S(2)}) collective-permute-start(bf16[2048,192]{0,1:T(8,128)(2,1)} %collective-permute-done.1), channel_id=1, source_target_pairs={{0,1},{1,2},{2,3},{3,4},{4,5},{5,6},{6,7},{8,9},{9,10},{10,11},{11... | collective-permute-start | bytes 2359304 | tf_op jit(solution)/shard_map/ppermute | solution.py:12
  140.6 10.2 %copy-start.11 = (s32[1,4]{1,0:T(1,128)S(1)}, s32[1,4]{1,0:T(1,128)}, u32[]{:S(2)}) copy-start(s32[1,4]{1,0:T(1,128)} %param.35) | copy-start | bytes 52
  160.7 21.2 %collective-permute-start.5 = (bf16[2048,192]{0,1:T(8,128)(2,1)}, bf16[2048,192]{0,1:T(8,128)(2,1)S(1)}, u32[]{:S(2)}, u32[]{:S(2)}) collective-permute-start(bf16[2048,192]{0,1:T(8,128)(2,1)} %collective-permute-done.4), channel_id=1, source_target_pairs={{1,0},{2,1},{3,2},{4,3},{5,4},{6,5},{7,6},{9,8},{10,9},{11,10},{12... | collective-permute-start | bytes 2359304 | tf_op jit(solution)/shard_map/ppermute | solution.py:12
  182.8 10.3 %copy-start.12 = (s32[1,8]{1,0:T(1,128)S(1)}, s32[1,8]{1,0:T(1,128)}, u32[]{:S(2)}) copy-start(s32[1,8]{1,0:T(1,128)} %param.33) | copy-start | bytes 100
  193.1 79.7 %copy-start.3 = (f32[2048,128]{0,1:T(8,128)S(1)}, f32[2048,128]{0,1:T(8,128)}, u32[]{:S(2)}) copy-start(f32[2048,128]{0,1:T(8,128)} %copy-done.2) | copy-start | bytes 3145732
  193.1 79.7 %copy-start.6 = (bf16[1,256,256]{2,1,0:T(8,128)(2,1)S(1)}, bf16[1,256,256]{2,1,0:T(8,128)(2,1)}, u32[]{:S(2)}) copy-start(bf16[1,256,256]{2,1,0:T(8,128)(2,1)} %param.30) | copy-start | bytes 393220
  193.1 79.7 %copy-start.7 = (f32[256,128]{0,1:T(8,128)S(1)}, f32[256,128]{0,1:T(8,128)}, u32[]{:S(2)}) copy-start(f32[256,128]{0,1:T(8,128)} %copy.41) | copy-start | bytes 393220
  193.2 79.7 %copy-start.10 = (f32[128]{0:T(128)S(1)}, f32[128]{0:T(128)}, u32[]{:S(2)}) copy-start(f32[128]{0:T(128)} %param.28) | copy-start | bytes 1540
where the time goes:
time: 281 us; the launch traced here: 279 us
  blocking collectives  84 us (30%)
  local copies, waits for them, and re-layouts  66.5 us (24%)
  matrix products  65 us (23%)
  starting transfers between devices  25.7 us (9%)
  other arithmetic  17.5 us (6%)
  loops' own time  12.3 us (4%)
  waiting for transfers between devices  7.31 us (3%)
    dot_general x7, matrix products, include(): jnp.dot(kernel_tile(points, other_points), other_values, preferred_elemen...  56.4 us
    ppermute x6, starting transfers between devices, passed_along(): return lax.ppermute(block, axis, route)  25.7 us
    psum x1, blocking collectives, body(): upper = lax.psum(upward_terms, 'leaf').astype(jnp.bfloat16)  25.1 us
    all_gather x1, blocking collectives, body(): skeletons = lax.all_gather(leaf_skeleton, 'leaf', axis=0, tiled=True)  20 us
    all_gather x1, blocking collectives, body(): values = lax.all_gather(coeffs[None], 'leaf', axis=0, tiled=True)  17.8 us
    reduce_sum x10, other arithmetic, kernel_tile(): right_sq = jnp.sum(right_f * right_f, axis=1)  14.6 us
    all_gather x1, blocking collectives, body(): values = lax.all_gather(upper[None], 'group', axis=0, tiled=True)  13.8 us
    unnamed x32, local copies, waits for them, and re-layouts  13.4 us
  transfers between devices with their start and end apart: 6, of which 1 were waited for; matrix products, arithmetic and copies ran while one was open for 19% of the time, Pallas kernels for 0%

commit v1 on v0

--- a/solution.py
+++ b/solution.py
@@ -107,7 +107,7 @@
     upward_terms = lax.dot_general(
         own_transfer, coeffs, (((0,), (0,)), ((), ())), preferred_element_type=jnp.float32
     )
-    upper = lax.psum(upward_terms, "leaf").astype(jnp.bfloat16)
+    upper = jnp.sum(lax.all_gather(upward_terms, axis_name="leaf"), axis=0).astype(jnp.bfloat16)
     cluster_row = cluster_far[0]
     skeletons = lax.all_gather(cluster_skeleton, "group", axis=0, tiled=True)
     values = lax.all_gather(upper[None], "group", axis=0, tiled=True)

time: 281 us -> 259 us (0.922)
  blocking collectives: 84 us -> 51.4 us
  between operations: 0.26 us -> 13.7 us
    psum x1 -> x0, blocking collectives: 25.1 us -> none  [body(): upper = lax.psum(upward_terms, 'leaf').astype(jnp.bfloat16)]
    all_gather x1, blocking collectives: 13.8 us -> 8.05 us  [body(): values = lax.all_gather(upper[None], 'group', axis=0, tiled=True)]
    unnamed x32 -> x37, local copies, waits for them, and re-layouts: 13.4 us -> 14.8 us
  transfers between devices with their start and end apart: 6 -> 7, of which waited for: 1 -> 1; matrix products, arithmetic and copies ran while one was open for 19% -> 19% of each run, Pallas kernels for 0% -> 0%
where the time goes in v1:
time: 259 us; the launch traced here: 257 us
  local copies, waits for them, and re-layouts  67.1 us (26%)
  matrix products  63.9 us (25%)
  blocking collectives  51.4 us (20%)
  starting transfers between devices  25.3 us (10%)
  other arithmetic  16.2 us (6%)
  between operations  13.7 us (5%)
  loops' own time  13.2 us (5%)
  waiting for transfers between devices  5.96 us (2%)
    dot_general x7, matrix products, include(): jnp.dot(kernel_tile(points, other_points), other_values, preferred_elemen...  56.3 us
    ppermute x6, starting transfers between devices, passed_along(): return lax.ppermute(block, axis, route)  25.3 us
    all_gather x1, blocking collectives, body(): skeletons = lax.all_gather(leaf_skeleton, 'leaf', axis=0, tiled=True)  20.3 us
    all_gather x1, blocking collectives, body(): values = lax.all_gather(coeffs[None], 'leaf', axis=0, tiled=True)  16.1 us
    unnamed x37, local copies, waits for them, and re-layouts  14.8 us
    reduce_sum x10, other arithmetic, kernel_tile(): right_sq = jnp.sum(right_f * right_f, axis=1)  12.9 us
    while x3, local copies, waits for them, and re-layouts, body(): lax.fori_loop(0, 2 * reach + 1, window_visit, jnp.zeros((leaf_rows, rhs_c...  12.1 us
    dynamic_slice x8, local copies, waits for them, and re-layouts, visit(): listed = lax.dynamic_index_in_dim(far_row, position, 0, keepdims=False)  10.6 us
  transfers between devices with their start and end apart: 7, of which 1 were waited for; matrix products, arithmetic and copies ran while one was open for 19% of the time, Pallas kernels for 0%

profile of v1, /device:TPU:15, one launch (start us, length us, event | category | flops | bytes accessed | tf_op | source)
XLA Modules:
  0.0 256.7 jit_solution(9671115431353544800)
XLA Ops:
  11.3 3.8 %collective-permute-start = (bf16[2048,192]{0,1:T(8,128)(2,1)}, bf16[2048,192]{0,1:T(8,128)(2,1)}, u32[]{:S(2)}, u32[]{:S(2)}) collective-permute-start(bf16[2048,192]{0,1:T(8,128)(2,1)} %pad_maximum_fusion), channel_id=1, source_target_pairs={{0,1},{1,2},{2,3},{3,4},{4,5},{5,6},{6,7},{8,9},{9,10},{10,11},{11... | collective-permute-start | bytes 2359304 | tf_op jit(solution)/shard_map/ppermute | solution.py:12
  18.4 5.9 %collective-permute-done = bf16[2048,192]{0,1:T(8,128)(2,1)} collective-permute-done((bf16[2048,192]{0,1:T(8,128)(2,1)}, bf16[2048,192]{0,1:T(8,128)(2,1)}, u32[]{:S(2)}, u32[]{:S(2)}) %collective-permute-start) | collective-permute-done | bytes 786464 | tf_op jit(solution)/shard_map/ppermute | solution.py:12
  24.3 4.4 %collective-permute-start.1 = (bf16[2048,192]{0,1:T(8,128)(2,1)}, bf16[2048,192]{0,1:T(8,128)(2,1)}, u32[]{:S(2)}, u32[]{:S(2)}) collective-permute-start(bf16[2048,192]{0,1:T(8,128)(2,1)} %collective-permute-done), channel_id=1, source_target_pairs={{0,1},{1,2},{2,3},{3,4},{4,5},{5,6},{6,7},{8,9},{9,10},{10,11},{11... | collective-permute-start | bytes 2359304 | tf_op jit(solution)/shard_map/ppermute | solution.py:12
  29.1 7.0 %all_gather.20 = bf16[4,256,64]{1,2,0:T(8,128)(2,1)} all-gather(bf16[1,256,64]{1,2,0:T(8,128)(2,1)S(1)} %copy-done.10), channel_id=1, replica_groups=mesh['group'=4,'leaf'=8] {'group'}, dimensions={0}, use_global_device_ids=true | all-gather | bytes 163840 | tf_op jit(solution)/shard_map/all_gather | solution.py:112
  38.7 16.1 %all-gather = bf16[2048,128]{1,0:T(8,128)(2,1)} all-gather(bf16[256,128]{1,0:T(8,128)(2,1)} %copy-done.6), channel_id=2, replica_groups=mesh['group'=4,'leaf'=8] {'leaf'}, dimensions={0}, use_global_device_ids=true | all-gather | bytes 589824 | tf_op jit(solution)/shard_map/all_gather | solution.py:105
  56.9 20.3 %all_gather.18 = bf16[8,256,64]{1,2,0:T(8,128)(2,1)} all-gather(bf16[1,256,64]{1,2,0:T(8,128)(2,1)} %param.31), channel_id=1, replica_groups=mesh['group'=4,'leaf'=8] {'leaf'}, dimensions={0}, use_global_device_ids=true | all-gather | bytes 294912 | tf_op jit(solution)/shard_map/all_gather | solution.py:104
  79.8 19.5 %while.50 = (s32[]{:T(128)}, f32[256,128]{1,0:T(8,128)}, s32[8]{0:T(128)}, bf16[1,256,64]{2,1,0:T(8,128)(2,1)S(1)}, bf16[8,256,64]{2,1,0:T(8,128)(2,1)}, /*index...) while((s32[]{:T(128)}, f32[256,128]{1,0:T(8,128)}, s32[8]{0:T(128)}, bf16[1,256,64]{2,1,0:T(8,128)(2,1)S(1)}, ...), condition=%wide.region_5.6_spmd, body=%wide.region_0.5_spmd.sunk | while | flops 25624072 | bytes 496837 | solution.py:106
  96.2 3.1 %conditional.6 = (f32[256,128]{1,0:T(8,128)}) conditional(s32[]{:T(128)} %bitcast.114, f32[256,128]{1,0:T(8,128)} %get-tuple-element.740, (bf16[1,256,64]{2,1,0:T(8,128)(2,1)S(1)}, s32[]{:T(128)}, bf16[8,256,64]{2,1,0:T(8,128)(2,1)}, bf16[8,256,128]{2,1,0:T(8,128)(2,1)}, f32[256,128]{1,0:T(8,128)}) %tuple.135), branch_computations={%region_1.1_spmd, %region_2.4_spmd} | conditional | flops 25624068 | bytes 496686 | solution.py:99
  100.9 7.8 %collective-permute-start.2 = (bf16[2048,192]{0,1:T(8,128)(2,1)}, bf16[2048,192]{0,1:T(8,128)(2,1)}, u32[]{:S(2)}, u32[]{:S(2)}) collective-permute-start(bf16[2048,192]{0,1:T(8,128)(2,1)} %collective-permute-done.1), channel_id=1, source_target_pairs={{0,1},{1,2},{2,3},{3,4},{4,5},{5,6},{6,7},{8,9},{9,10},{10,11},{11... | collective-permute-start | bytes 2359304 | tf_op jit(solution)/shard_map/ppermute | solution.py:12
  108.8 7.6 %gather_fusion = f32[2048,128]{1,0:T(8,128)} fusion(f32[2048,128]{1,0:T(8,128)S(1)} %copy-done.1, s32[2048]{0:T(1024)S(1)} %broadcast_clamp_fusion), kind=kCustom, calls=%fused_computation | custom fusion | bytes 2105344 | tf_op jit(solution)/shard_map/gather | solution.py:132
  116.4 2.6 %copy.43 = f32[2048,128]{0,1:T(8,128)} copy(f32[2048,128]{1,0:T(8,128)} %gather_fusion) | data formatting | bytes 2097152 | tf_op jit(solution)/shard_map/gather | solution.py:132
  119.0 5.4 %collective-permute-start.5 = (bf16[2048,192]{0,1:T(8,128)(2,1)}, bf16[2048,192]{0,1:T(8,128)(2,1)}, u32[]{:S(2)}, u32[]{:S(2)}) collective-permute-start(bf16[2048,192]{0,1:T(8,128)(2,1)} %collective-permute-done.4), channel_id=1, source_target_pairs={{1,0},{2,1},{3,2},{4,3},{5,4},{6,5},{7,6},{9,8},{10,9},{11,10},{12... | collective-permute-start | bytes 2359304 | tf_op jit(solution)/shard_map/ppermute | solution.py:12
  126.2 8.0 %all-gather.2 = bf16[1024,128]{0,1:T(8,128)(2,1)S(1)} all-gather(bf16[256,128]{0,1:T(8,128)(2,1)S(1)} %bitcast_reduce_fusion), channel_id=4, replica_groups=mesh['group'=4,'leaf'=8] {'group'}, dimensions={0}, use_global_device_ids=true | all-gather | bytes 327680 | tf_op jit(solution)/shard_map/all_gather | solution.py:113
  134.5 6.3 %while.51 = (s32[]{:T(128)}, f32[256,128]{1,0:T(8,128)S(1)}, s32[4]{0:T(128)S(1)}, bf16[1,256,64]{2,1,0:T(8,128)(2,1)S(1)}, bf16[4,256,64]{2,1,0:T(8,128)(2,1)S(...) while((s32[]{:T(128)}, f32[256,128]{1,0:T(8,128)S(1)}, s32[4]{0:T(128)S(1)}, ...), condition=%wide.region_12.13_spmd, body=%wide.region_7.12_spmd.sunk | while | flops 25624072 | bytes 529605 | solution.py:127
  154.4 9.3 %copy.41 = bf16[14336,192]{1,0:T(8,128)(2,1)} copy(bf16[14336,192]{0,1:T(8,128)(2,1)} %constant_dynamic-update-slice_fusion) | data formatting | bytes 11010048 | tf_op jit(solution)/shard_map/while | solution.py:83
  164.8 76.8 %while.52 = (s32[]{:T(128)}, f32[2048,128]{1,0:T(8,128)}, s32[]{:T(128)}, s32[8]{0:T(128)S(1)}, bf16[2048,64]{1,0:T(8,128)(2,1)S(1)}, /*index=5*/bf16[14336,192]...) while((s32[]{:T(128)}, f32[2048,128]{1,0:T(8,128)}, ...), condition=%wide.region_18.19_spmd, body=%wide.region_13.18_spmd.sunk | while | flops 1632628736 | bytes 3966781 | solution.py:83
  166.0 9.7 %conditional.8 = (f32[2048,128]{1,0:T(8,128)}) conditional(s32[]{:T(128)} %convert_element_type.127, f32[2048,128]{1,0:T(8,128)} %get-tuple-element.708, (bf16[2048,64]{1,0:T(8,128)(2,1)S(1)}, s32[]{:T(128)}, bf16[14336,192]{1,0:T(8,128)(2,1)}, f32[2048,128]{1,0:T(8,128)}) %tuple.139), branch_computations={%region_14.14_spmd, %region_15.17_spmd} | conditional | flops 1632628736 | bytes 3966534 | solution.py:81
  167.7 8.0 %convolution_add_fusion = f32[2048,128]{1,0:T(8,128)} fusion(f32[2048,128]{1,0:T(8,128)} %get-tuple-element.471, bf16[2048,64]{1,0:T(8,128)(2,1)S(1)} %get-tuple-element.472, f32[2048]{0:T(1024)S(1)} %get-tuple-element.582, f32[2048]{0:T(1024)S(1)} %get-tuple-element.583, bf16[14336,192]{1,0:T(8,128)(2,1)} %get-tuple-element.473, s32[]{:T(128)S(6)} %select_n.45, ...), kind=kOutput, calls=%fused_computation.47 | convolution fusion | flops 1631846400 | bytes 3425792 | tf_op jit(solution)/shard_map/while/body/eval_jaxpr/cond/branch_1_fun/dot_general | solution.py:77
  177.0 9.7 %conditional.8 = (f32[2048,128]{1,0:T(8,128)}) conditional(s32[]{:T(128)} %convert_element_type.127, f32[2048,128]{1,0:T(8,128)} %get-tuple-element.708, (bf16[2048,64]{1,0:T(8,128)(2,1)S(1)}, s32[]{:T(128)}, bf16[14336,192]{1,0:T(8,128)(2,1)}, f32[2048,128]{1,0:T(8,128)}) %tuple.139), branch_computations={%region_14.14_spmd, %region_15.17_spmd} | conditional | flops 1632628736 | bytes 3966534 | solution.py:81
  178.7 8.0 %convolution_add_fusion = f32[2048,128]{1,0:T(8,128)} fusion(f32[2048,128]{1,0:T(8,128)} %get-tuple-element.471, bf16[2048,64]{1,0:T(8,128)(2,1)S(1)} %get-tuple-element.472, f32[2048]{0:T(1024)S(1)} %get-tuple-element.582, f32[2048]{0:T(1024)S(1)} %get-tuple-element.583, bf16[14336,192]{1,0:T(8,128)(2,1)} %get-tuple-element.473, s32[]{:T(128)S(6)} %select_n.45, ...), kind=kOutput, calls=%fused_computation.47 | convolution fusion | flops 1631846400 | bytes 3425792 | tf_op jit(solution)/shard_map/while/body/eval_jaxpr/cond/branch_1_fun/dot_general | solution.py:77
  188.0 9.7 %conditional.8 = (f32[2048,128]{1,0:T(8,128)}) conditional(s32[]{:T(128)} %convert_element_type.127, f32[2048,128]{1,0:T(8,128)} %get-tuple-element.708, (bf16[2048,64]{1,0:T(8,128)(2,1)S(1)}, s32[]{:T(128)}, bf16[14336,192]{1,0:T(8,128)(2,1)}, f32[2048,128]{1,0:T(8,128)}) %tuple.139), branch_computations={%region_14.14_spmd, %region_15.17_spmd} | conditional | flops 1632628736 | bytes 3966534 | solution.py:81
  189.6 8.0 %convolution_add_fusion = f32[2048,128]{1,0:T(8,128)} fusion(f32[2048,128]{1,0:T(8,128)} %get-tuple-element.471, bf16[2048,64]{1,0:T(8,128)(2,1)S(1)} %get-tuple-element.472, f32[2048]{0:T(1024)S(1)} %get-tuple-element.582, f32[2048]{0:T(1024)S(1)} %get-tuple-element.583, bf16[14336,192]{1,0:T(8,128)(2,1)} %get-tuple-element.473, s32[]{:T(128)S(6)} %select_n.45, ...), kind=kOutput, calls=%fused_computation.47 | convolution fusion | flops 1631846400 | bytes 3425792 | tf_op jit(solution)/shard_map/while/body/eval_jaxpr/cond/branch_1_fun/dot_general | solution.py:77
  198.9 9.7 %conditional.8 = (f32[2048,128]{1,0:T(8,128)}) conditional(s32[]{:T(128)} %convert_element_type.127, f32[2048,128]{1,0:T(8,128)} %get-tuple-element.708, (bf16[2048,64]{1,0:T(8,128)(2,1)S(1)}, s32[]{:T(128)}, bf16[14336,192]{1,0:T(8,128)(2,1)}, f32[2048,128]{1,0:T(8,128)}) %tuple.139), branch_computations={%region_14.14_spmd, %region_15.17_spmd} | conditional | flops 1632628736 | bytes 3966534 | solution.py:81
  200.6 8.0 %convolution_add_fusion = f32[2048,128]{1,0:T(8,128)} fusion(f32[2048,128]{1,0:T(8,128)} %get-tuple-element.471, bf16[2048,64]{1,0:T(8,128)(2,1)S(1)} %get-tuple-element.472, f32[2048]{0:T(1024)S(1)} %get-tuple-element.582, f32[2048]{0:T(1024)S(1)} %get-tuple-element.583, bf16[14336,192]{1,0:T(8,128)(2,1)} %get-tuple-element.473, s32[]{:T(128)S(6)} %select_n.45, ...), kind=kOutput, calls=%fused_computation.47 | convolution fusion | flops 1631846400 | bytes 3425792 | tf_op jit(solution)/shard_map/while/body/eval_jaxpr/cond/branch_1_fun/dot_general | solution.py:77
  209.9 9.7 %conditional.8 = (f32[2048,128]{1,0:T(8,128)}) conditional(s32[]{:T(128)} %convert_element_type.127, f32[2048,128]{1,0:T(8,128)} %get-tuple-element.708, (bf16[2048,64]{1,0:T(8,128)(2,1)S(1)}, s32[]{:T(128)}, bf16[14336,192]{1,0:T(8,128)(2,1)}, f32[2048,128]{1,0:T(8,128)}) %tuple.139), branch_computations={%region_14.14_spmd, %region_15.17_spmd} | conditional | flops 1632628736 | bytes 3966534 | solution.py:81
  211.6 8.0 %convolution_add_fusion = f32[2048,128]{1,0:T(8,128)} fusion(f32[2048,128]{1,0:T(8,128)} %get-tuple-element.471, bf16[2048,64]{1,0:T(8,128)(2,1)S(1)} %get-tuple-element.472, f32[2048]{0:T(1024)S(1)} %get-tuple-element.582, f32[2048]{0:T(1024)S(1)} %get-tuple-element.583, bf16[14336,192]{1,0:T(8,128)(2,1)} %get-tuple-element.473, s32[]{:T(128)S(6)} %select_n.45, ...), kind=kOutput, calls=%fused_computation.47 | convolution fusion | flops 1631846400 | bytes 3425792 | tf_op jit(solution)/shard_map/while/body/eval_jaxpr/cond/branch_1_fun/dot_general | solution.py:77
  220.8 9.7 %conditional.8 = (f32[2048,128]{1,0:T(8,128)}) conditional(s32[]{:T(128)} %convert_element_type.127, f32[2048,128]{1,0:T(8,128)} %get-tuple-element.708, (bf16[2048,64]{1,0:T(8,128)(2,1)S(1)}, s32[]{:T(128)}, bf16[14336,192]{1,0:T(8,128)(2,1)}, f32[2048,128]{1,0:T(8,128)}) %tuple.139), branch_computations={%region_14.14_spmd, %region_15.17_spmd} | conditional | flops 1632628736 | bytes 3966534 | solution.py:81
  222.5 8.0 %convolution_add_fusion = f32[2048,128]{1,0:T(8,128)} fusion(f32[2048,128]{1,0:T(8,128)} %get-tuple-element.471, bf16[2048,64]{1,0:T(8,128)(2,1)S(1)} %get-tuple-element.472, f32[2048]{0:T(1024)S(1)} %get-tuple-element.582, f32[2048]{0:T(1024)S(1)} %get-tuple-element.583, bf16[14336,192]{1,0:T(8,128)(2,1)} %get-tuple-element.473, s32[]{:T(128)S(6)} %select_n.45, ...), kind=kOutput, calls=%fused_computation.47 | convolution fusion | flops 1631846400 | bytes 3425792 | tf_op jit(solution)/shard_map/while/body/eval_jaxpr/cond/branch_1_fun/dot_general | solution.py:77
  231.8 9.8 %conditional.8 = (f32[2048,128]{1,0:T(8,128)}) conditional(s32[]{:T(128)} %convert_element_type.127, f32[2048,128]{1,0:T(8,128)} %get-tuple-element.708, (bf16[2048,64]{1,0:T(8,128)(2,1)S(1)}, s32[]{:T(128)}, bf16[14336,192]{1,0:T(8,128)(2,1)}, f32[2048,128]{1,0:T(8,128)}) %tuple.139), branch_computations={%region_14.14_spmd, %region_15.17_spmd} | conditional | flops 1632628736 | bytes 3966534 | solution.py:81
  233.5 8.1 %convolution_add_fusion = f32[2048,128]{1,0:T(8,128)} fusion(f32[2048,128]{1,0:T(8,128)} %get-tuple-element.471, bf16[2048,64]{1,0:T(8,128)(2,1)S(1)} %get-tuple-element.472, f32[2048]{0:T(1024)S(1)} %get-tuple-element.582, f32[2048]{0:T(1024)S(1)} %get-tuple-element.583, bf16[14336,192]{1,0:T(8,128)(2,1)} %get-tuple-element.473, s32[]{:T(128)S(6)} %select_n.45, ...), kind=kOutput, calls=%fused_computation.47 | convolution fusion | flops 1631846400 | bytes 3425792 | tf_op jit(solution)/shard_map/while/body/eval_jaxpr/cond/branch_1_fun/dot_general | solution.py:77
  241.6 2.5 copy.42
  244.2 3.2 %fusion.56 = f32[2048,128]{0,1:T(8,128)} fusion(f32[2048,128]{0,1:T(8,128)S(1)} %copy-done.3, f32[2048,128]{0,1:T(8,128)} %copy.43, f32[2048,128]{0,1:T(8,128)} %copy.42, bf16[2048,256]{1,0:T(8,128)(2,1)S(1)} %copy-done, f32[256,128]{0,1:T(8,128)S(1)} %copy-done.9, f32[128]{0:T(128)S(1)} %copy-done.12, bf16[1,256,256]{2,1,0:T(8,128)(2,1)S(1)} %copy-done.8, ...), kind=kOutput, calls=%fused_computation.58 | convolution fusion | flops 152141824 | bytes 5636608 | tf_op jit(solution)/shard_map/dot_general | solution.py:131
  (110 shorter events, 71.1 us)
Async XLA Ops:
  6.5 8.5 %copy-start = (bf16[2048,256]{1,0:T(8,128)(2,1)S(1)}, bf16[2048,256]{1,0:T(8,128)(2,1)}, u32[]{:S(2)}) copy-start(bf16[2048,256]{1,0:T(8,128)(2,1)} %param.29) | copy-start | bytes 3145732
  6.5 22.1 %copy-start.4 = (bf16[2048,64]{0,1:T(8,128)(2,1)S(1)}, bf16[2048,64]{0,1:T(8,128)(2,1)}, u32[]{:S(2)}) copy-start(bf16[2048,64]{0,1:T(8,128)(2,1)} %param.24) | copy-start | bytes 786436
  6.5 9.0 %copy-start.7 = (bf16[1,256,256]{2,1,0:T(8,128)(2,1)S(1)}, bf16[1,256,256]{2,1,0:T(8,128)(2,1)}, u32[]{:S(2)}) copy-start(bf16[1,256,256]{2,1,0:T(8,128)(2,1)} %param.30) | copy-start | bytes 393220
  6.5 22.4 %copy-start.10 = (bf16[1,256,64]{1,2,0:T(8,128)(2,1)S(1)}, bf16[1,256,64]{1,2,0:T(8,128)(2,1)}, u32[]{:S(2)}) copy-start(bf16[1,256,64]{1,2,0:T(8,128)(2,1)} %param.32) | copy-start | bytes 98308
  6.5 117.8 %all-gather.5.cloned.1.call-start = ((), (), s32[]{:S(2)}) async-start(), calls=%async_computation | async-start | bytes 1179648 | tf_op jit(solution)/shard_map/all_gather | solution.py:110
  8.3 1.0 copy-start.2
  9.3 99.5 %copy-start.11 = (s32[1,2048]{1,0:T(1,128)S(1)}, s32[1,2048]{1,0:T(1,128)}, u32[]{:S(2)}) copy-start(s32[1,2048]{1,0:T(1,128)} %param.25) | copy-start | bytes 24580
  9.3 99.5 %copy-start.1 = (f32[2048,128]{1,0:T(8,128)S(1)}, f32[2048,128]{1,0:T(8,128)}, u32[]{:S(2)}) copy-start(f32[2048,128]{1,0:T(8,128)} %param.27) | copy-start | bytes 3145732
  11.3 13.0 %collective-permute-start = (bf16[2048,192]{0,1:T(8,128)(2,1)}, bf16[2048,192]{0,1:T(8,128)(2,1)}, u32[]{:S(2)}, u32[]{:S(2)}) collective-permute-start(bf16[2048,192]{0,1:T(8,128)(2,1)} %pad_maximum_fusion), channel_id=1, source_target_pairs={{0,1},{1,2},{2,3},{3,4},{4,5},{5,6},{6,7},{8,9},{9,10},{10,11},{11... | collective-permute-start | bytes 2359304 | tf_op jit(solution)/shard_map/ppermute | solution.py:12
  15.6 13.4 %copy-start.6 = (bf16[256,128]{1,0:T(8,128)(2,1)}, bf16[256,128]{1,0:T(8,128)(2,1)S(1)}, u32[]{:S(2)}) copy-start(bf16[256,128]{1,0:T(8,128)(2,1)S(1)} %convolution_convert_fusion) | copy-start | bytes 196612
  16.5 38.4 %collective-permute-start.3 = (bf16[2048,192]{0,1:T(8,128)(2,1)}, bf16[2048,192]{0,1:T(8,128)(2,1)}, u32[]{:S(2)}, u32[]{:S(2)}) collective-permute-start(bf16[2048,192]{0,1:T(8,128)(2,1)} %pad_maximum_fusion), channel_id=1, source_target_pairs={{1,0},{2,1},{3,2},{4,3},{5,4},{6,5},{7,6},{9,8},{10,9},{11,10},{12... | collective-permute-start | bytes 2359304 | tf_op jit(solution)/shard_map/ppermute | solution.py:12
  24.3 76.6 %collective-permute-start.1 = (bf16[2048,192]{0,1:T(8,128)(2,1)}, bf16[2048,192]{0,1:T(8,128)(2,1)}, u32[]{:S(2)}, u32[]{:S(2)}) collective-permute-start(bf16[2048,192]{0,1:T(8,128)(2,1)} %collective-permute-done), channel_id=1, source_target_pairs={{0,1},{1,2},{2,3},{3,4},{4,5},{5,6},{6,7},{8,9},{9,10},{10,11},{11... | collective-permute-start | bytes 2359304 | tf_op jit(solution)/shard_map/ppermute | solution.py:12
  54.8 64.1 %collective-permute-start.4 = (bf16[2048,192]{0,1:T(8,128)(2,1)}, bf16[2048,192]{0,1:T(8,128)(2,1)}, u32[]{:S(2)}, u32[]{:S(2)}) collective-permute-start(bf16[2048,192]{0,1:T(8,128)(2,1)} %collective-permute-done.3), channel_id=1, source_target_pairs={{1,0},{2,1},{3,2},{4,3},{5,4},{6,5},{7,6},{9,8},{10,9},{11,10},{12... | collective-permute-start | bytes 2359304 | tf_op jit(solution)/shard_map/ppermute | solution.py:12
  100.9 39.8 %collective-permute-start.2 = (bf16[2048,192]{0,1:T(8,128)(2,1)}, bf16[2048,192]{0,1:T(8,128)(2,1)}, u32[]{:S(2)}, u32[]{:S(2)}) collective-permute-start(bf16[2048,192]{0,1:T(8,128)(2,1)} %collective-permute-done.1), channel_id=1, source_target_pairs={{0,1},{1,2},{2,3},{3,4},{4,5},{5,6},{6,7},{8,9},{9,10},{10,11},{11... | collective-permute-start | bytes 2359304 | tf_op jit(solution)/shard_map/ppermute | solution.py:12
  116.4 18.1 %copy-start.5 = (bf16[4,256,64]{2,1,0:T(8,128)(2,1)S(1)}, bf16[4,256,64]{2,1,0:T(8,128)(2,1)}, u32[]{:S(2)}) copy-start(bf16[4,256,64]{2,1,0:T(8,128)(2,1)} %copy.37) | copy-start | bytes 393220
  116.4 18.1 %copy-start.13 = (s32[1,4]{1,0:T(1,128)S(1)}, s32[1,4]{1,0:T(1,128)}, u32[]{:S(2)}) copy-start(s32[1,4]{1,0:T(1,128)} %param.35) | copy-start | bytes 52
  119.0 33.3 %collective-permute-start.5 = (bf16[2048,192]{0,1:T(8,128)(2,1)}, bf16[2048,192]{0,1:T(8,128)(2,1)}, u32[]{:S(2)}, u32[]{:S(2)}) collective-permute-start(bf16[2048,192]{0,1:T(8,128)(2,1)} %collective-permute-done.4), channel_id=1, source_target_pairs={{1,0},{2,1},{3,2},{4,3},{5,4},{6,5},{7,6},{9,8},{10,9},{11,10},{12... | collective-permute-start | bytes 2359304 | tf_op jit(solution)/shard_map/ppermute | solution.py:12
  154.4 10.4 %copy-start.14 = (s32[1,8]{1,0:T(1,128)S(1)}, s32[1,8]{1,0:T(1,128)}, u32[]{:S(2)}) copy-start(s32[1,8]{1,0:T(1,128)} %param.33) | copy-start | bytes 100
  164.7 79.4 %copy-start.3 = (f32[2048,128]{0,1:T(8,128)S(1)}, f32[2048,128]{0,1:T(8,128)}, u32[]{:S(2)}) copy-start(f32[2048,128]{0,1:T(8,128)} %copy-done.2) | copy-start | bytes 3145732
  164.7 79.4 %copy-start.8 = (bf16[1,256,256]{2,1,0:T(8,128)(2,1)S(1)}, bf16[1,256,256]{2,1,0:T(8,128)(2,1)}, u32[]{:S(2)}) copy-start(bf16[1,256,256]{2,1,0:T(8,128)(2,1)} %param.30) | copy-start | bytes 393220
  164.7 79.4 %copy-start.9 = (f32[256,128]{0,1:T(8,128)S(1)}, f32[256,128]{0,1:T(8,128)}, u32[]{:S(2)}) copy-start(f32[256,128]{0,1:T(8,128)} %copy.39) | copy-start | bytes 393220
  164.7 79.4 %copy-start.12 = (f32[128]{0:T(128)S(1)}, f32[128]{0:T(128)}, u32[]{:S(2)}) copy-start(f32[128]{0:T(128)} %param.28) | copy-start | bytes 1540
Sparse Core Ops, SparseCore 0:
  16.6 24.4 all-gather.4
